TPU v7x, 32 devices: a whole 2x2x4 slice. The times are simulated.
32 devices in a mesh: tm: 2 (over y), space: 16 (over z, x, core).
Axes of the slice: x: 2, y: 2, z: 4, core: 2. Of those that a mesh axis runs over, the one named last changes fastest.
Arguments:
- control: float32 [32, 51200], P(('tm', 'space')), may hold values from -4 to 4
- spectrum: float32 [51200], replicated, may hold values from 0.2 to 2
- perturb: bfloat16 [4, 32, 4, 51200], P('tm', None, None, 'space'), may hold values from -1 to 1
- obs_index: int32 [4, 32768], P('tm', 'space'), may hold values from 0 to 12799
- innovation: float32 [4, 32768], P('tm', 'space'), may hold values from -10 to 10
- obs_sigma: float32 [4, 32768], P('tm', 'space'), may hold values from 0.5 to 2
- qc_class: int32 [4, 32768], P('tm', 'space'), may hold values from 0 to 2
Outputs:
- control_out: float32 [32, 51200], P(('tm', 'space'))
- cost_list: float32 [1], replicated
Inputs may be any that keep to these rules, and one draw needn't show every extreme that they name: `obs_index`: observation o of block o // 2048 observes the cell level * 3200 + point, the point counted within the block's piece of the grid; repeats may occur.
All inputs are finite; a program needn't handle non-finite values.
Results may differ from a plain program's by a relative error of at most 0.0034.
Values may be sent and summed in bfloat16 or wider, within the bound.
A program may use at most 128 MiB of HBM per device.

v0:
```python
import jax
import jax.numpy as jnp
from jax import lax
from jax.sharding import PartitionSpec as P

GX = 320
GY = 160


def lookup_tables(segment_length):
    wave_num = jnp.arange(segment_length, dtype=jnp.float32)[:, None]
    grid_positions = jnp.arange(segment_length, dtype=jnp.float32)[None, :]
    basis = jnp.cos(jnp.pi * (grid_positions + 0.5) * wave_num / segment_length) * jnp.sqrt(
        2.0 / segment_length
    )
    return jnp.where(wave_num == 0, basis * jnp.sqrt(0.5), basis)


def synthesize(control, spectrum, basis_x, basis_y):
    coeffs = (control * spectrum[None, :]).reshape(control.shape[0], GX, GY)
    middle = jnp.einsum("kn,mkl->mnl", basis_x, coeffs, precision=lax.Precision.HIGHEST)
    result = jnp.einsum("mnl,lp->mnp", middle, basis_y, precision=lax.Precision.HIGHEST)
    return result.reshape(control.shape[0], GX * GY)


def analyze(adjoint, spectrum, basis_x, basis_y):
    state_fields = adjoint.reshape(adjoint.shape[0], GX, GY)
    middle = jnp.einsum("kn,mnp->mkp", basis_x, state_fields, precision=lax.Precision.HIGHEST)
    result = jnp.einsum("mkp,lp->mkl", middle, basis_y, precision=lax.Precision.HIGHEST)
    return result.reshape(adjoint.shape[0], GX * GY) * spectrum[None, :]


def per_device(control, spectrum, perturb, obs_index, innovation, obs_sigma, qc_class):
    basis_x = lookup_tables(GX)
    basis_y = lookup_tables(GY)
    slot_count = perturb.shape[0]
    levels = perturb.shape[2]
    piece_len = perturb.shape[3]
    radius = jnp.where(qc_class == 0, 4.0, jnp.where(qc_class == 1, 2.0, 1.0)).astype(jnp.float32)

    def scatter_cells(indices, values):
        return jnp.zeros((levels * piece_len,), jnp.float32).at[indices].add(values)

    member_field = synthesize(control, spectrum, basis_x, basis_y).astype(jnp.bfloat16)
    pieces = lax.all_to_all(member_field, "space", split_axis=1, concat_axis=0, tiled=True)
    selected_entries = perturb
    increment = jnp.einsum(
        "dzab,zb->dab",
        selected_entries,
        lax.all_gather(pieces, "tm", axis=0, tiled=True),
        preferred_element_type=jnp.float32,
    )
    cells_flat = increment.reshape(slot_count, levels * piece_len)
    modelled = jnp.take_along_axis(cells_flat, obs_index, axis=1)
    scaled = (modelled - innovation) / obs_sigma
    scaled_sq = scaled * scaled / (radius * radius)
    obs_part = jnp.sum(0.5 * radius * radius * jnp.log1p(scaled_sq))
    back_part = 0.5 * jnp.sum(control * control)
    obs_grad = scaled / ((1.0 + scaled_sq) * obs_sigma)
    control_update = jax.vmap(scatter_cells)(obs_index, obs_grad).astype(jnp.bfloat16)
    control_update = control_update.reshape(slot_count, levels, piece_len)
    selected_entries = perturb
    summed_rows = lax.psum_scatter(
        jnp.einsum(
            "qiyr,qyr->ir", selected_entries, control_update, preferred_element_type=jnp.float32
        ).astype(jnp.bfloat16),
        "tm",
        scatter_dimension=0,
        tiled=True,
    ).astype(jnp.float32)
    adjoint = lax.all_to_all(
        summed_rows.astype(jnp.bfloat16), "space", split_axis=0, concat_axis=1, tiled=True
    ).astype(summed_rows.dtype)
    gradient = control + analyze(adjoint, spectrum, basis_x, basis_y)
    grad_part = jnp.sum(gradient * gradient)
    obs_cost, back_cost = lax.psum((obs_part, back_part), ("tm", "space"))
    grad_sq = lax.psum(grad_part, ("tm", "space"))
    total_cost = back_cost + obs_cost
    step_size = 0.5 * total_cost / (grad_sq + 1e-06)
    control = control - step_size * gradient
    cost_list = [total_cost]
    return (control, jnp.stack(cost_list))


def solution(mesh):
    in_specs = (
        P(("tm", "space"), None),
        P(),
        P("tm", None, None, "space"),
        P("tm", "space"),
        P("tm", "space"),
        P("tm", "space"),
        P("tm", "space"),
    )
    out_specs = (P(("tm", "space"), None), P())
    return jax.shard_map(
        per_device, mesh=mesh, in_specs=in_specs, out_specs=out_specs, check_vma=False
    )
```

profile of v0, /device:TPU:12, one launch (start us, length us, event | category | flops | bytes accessed | tf_op | source)
XLA Modules:
  0.0 175.2 jit_solution(5619311376740743592)
XLA Ops:
  7.2 2.4 %multiply_reduce_fusion.4 = (f32[]{:T(128)}, f32[51200]{0:T(1024)S(1)}) fusion(f32[1,51200]{1,0:T(1,128)} %param.7, f32[1,51200]{1,0:T(1,128)} %bitcast.56), kind=kLoop, calls=%fused_computation.23 | loop fusion | flops 153599 | bytes 614404 | tf_op jit(solution)/shard_map/reduce_sum | solution.py:58
  9.6 0.1 reshape.98
  9.8 2.6 %convolution_bitcast_fusion.1 = f32[320,160]{0,1:T(8,128)S(1)} fusion(f32[320,160]{1,0:T(8,128)S(1)} %reshape.98, f32[320]{0:T(512)S(1)} %add_multiply_fusion, pred[320]{0:T(512)(128)(4,1)S(1)} %iota_compare_fusion), kind=kOutput, calls=%fused_computation.5 | convolution fusion | flops 197120000 | bytes 411200 | tf_op jit(solution)/shard_map/kn,mkl->mnl/dot_general | solution.py:21
  12.4 1.1 convolution_convert_fusion
  13.4 0.0 copy-start
  13.5 0.1 copy.14
  13.6 0.3 convert_element_type.33
  13.9 0.5 broadcast.94
  14.4 1.2 reduce.13
  15.5 0.8 reshape.139
  16.3 6.3 %all-to-all-start = ((bf16[16,2,1600]{2,1,0:T(2,128)(2,1)}), bf16[16,2,1600]{2,1,0:T(2,128)(2,1)S(1)}, u32[]{:S(2)}, u32[]{:S(2)}) async-start(bf16[16,2,1600]{2,1,0:T(2,128)(2,1)} %reshape.139), calls=%async_computation | async-start | bytes 212992 | tf_op jit(solution)/shard_map/all_to_all | solution.py:45
  22.6 0.0 reduce-scatter.2.cloned.1.call-start
  22.7 0.0 copy-done.3
  22.7 0.0 copy-done.7
  22.7 0.1 multiply_reduce_fusion.5
  22.8 0.0 copy-done.8
  22.8 0.1 and_reduce_fusion
  23.0 4.9 %all-to-all-done = bf16[16,2,1600]{2,1,0:T(2,128)(2,1)S(1)} async-done(((bf16[16,2,1600]{2,1,0:T(2,128)(2,1)}), bf16[16,2,1600]{2,1,0:T(2,128)(2,1)S(1)}, u32[]{:S(2)}, u32[]{:S(2)}) %all-to-all-start) | async-done | bytes 102432 | tf_op jit(solution)/shard_map/all_to_all | solution.py:45
  27.9 0.2 reshape.140
  28.1 5.8 %all-gather = bf16[1,32,3200]{2,1,0:T(8,128)(2,1)S(1)} all-gather(bf16[1,16,3200]{2,1,0:T(8,128)(2,1)S(1)} %copy.16), channel_id=2, replica_groups=mesh['tm'=2,'space'=16] {'tm'}, dimensions={1}, use_global_device_ids=true | all-gather | bytes 307200 | tf_op jit(solution)/shard_map/all_gather | solution.py:50
  34.0 0.0 copy-done
  34.0 0.9 multiply_reduce_fusion.1
  34.8 0.1 copy.36
  34.9 0.0 copy-start.4
  34.9 0.0 copy-start.5
  34.9 0.0 copy-start.6
  34.9 34.9 %gather_fusion = f32[4096]{0:T(1024)S(1)} fusion(f32[2,12800]{1,0:T(2,128)S(1)} %bitcast.52, s32[4096]{0:T(1024)S(1)} %bitcast.53), kind=kCustom, calls=%fused_computation | custom fusion | bytes 65536 | tf_op jit(solution)/shard_map/jit(take_along_axis)/gather | solution.py:54
  69.9 0.0 copy-done.4
  69.9 0.0 copy-done.5
  69.9 0.8 fusion.26
  70.7 21.9 %scatter_custom_fusion = f32[25600]{0:T(1024)S(1)} fusion(s32[4096]{0:T(1024)S(1)} %bitcast.61, f32[4096]{0:T(1024)S(1)} %bitcast.62, f32[]{:T(128)} %constant.17.clone.1), kind=kCustom, calls=%fused_computation.39 | custom fusion | flops 4096 | bytes 102404
  92.7 2.2 %multiply_reduce_fusion = bf16[3200,32]{0,1:T(8,128)(2,1)} fusion(f32[3200,2,4]{0,2,1:T(4,128)S(1)} %bitcast_convert_fusion.1, bf16[2,32,4,3200]{3,2,1,0:T(4,128)(2,1)S(1)} %copy-done), kind=kLoop, calls=%fused_computation.2 | loop fusion | flops 2355200 | bytes 1945600 | tf_op jit(solution)/shard_map/qiyr,qyr->ir/dot_general | solution.py:64
  94.9 0.0 reduce-scatter.2.cloned.1.call-update
  94.9 9.4 %reduce-scatter.2.cloned.1.call-done = bf16[16,3200]{1,0:T(8,128)(2,1)} async-done(((bf16[32,3200]{1,0:T(8,128)(2,1)}), bf16[16,3200]{1,0:T(8,128)(2,1)}) %reduce-scatter.2.cloned.1.call-update) | async-done | bytes 102416 | tf_op jit(solution)/shard_map/reduce_scatter | solution.py:63
  104.3 1.5 reduce.14
  105.8 0.8 reshape.141
  106.6 6.2 %all-to-all-start.1 = ((bf16[16,2,1600]{2,1,0:T(2,128)(2,1)}), bf16[16,2,1600]{2,1,0:T(2,128)(2,1)S(1)}, u32[]{:S(2)}, u32[]{:S(2)}) async-start(bf16[16,2,1600]{2,1,0:T(2,128)(2,1)} %reshape.141), calls=%async_computation.2 | async-start | bytes 212992 | tf_op jit(solution)/shard_map/all_to_all | solution.py:71
  114.2 3.9 %all-to-all-done.1 = bf16[16,2,1600]{2,1,0:T(2,128)(2,1)S(1)} async-done(((bf16[16,2,1600]{2,1,0:T(2,128)(2,1)}), bf16[16,2,1600]{2,1,0:T(2,128)(2,1)S(1)}, u32[]{:S(2)}, u32[]{:S(2)}) %all-to-all-start.1) | async-done | bytes 102432 | tf_op jit(solution)/shard_map/all_to_all | solution.py:71
  118.1 0.2 reshape.142
  118.3 0.0 copy-start.1
  118.3 0.6 reduce.5
  118.9 0.2 reshape.103
  119.1 2.3 %convolution_bitcast_fusion = f32[320,160]{0,1:T(8,128)S(1)} fusion(bf16[320,160]{1,0:T(8,128)(2,1)S(1)} %reshape.103, f32[320]{0:T(512)S(1)} %add_multiply_fusion, pred[320]{0:T(512)(128)(4,1)S(1)} %iota_compare_fusion), kind=kOutput, calls=%fused_computation.4 | convolution fusion | flops 197120000 | bytes 308800 | tf_op jit(solution)/shard_map/kn,mnp->mkp/dot_general | solution.py:28
  121.4 1.3 fusion.10
  122.7 0.3 reshape.105
  123.0 1.0 multiply_reduce_fusion.2
  124.1 42.1 %all-reduce = (f32[]{:T(128)}, f32[]{:T(128)}) all-reduce(f32[]{:T(128)S(6)} %add.65, f32[]{:T(128)} %get-tuple-element.6), channel_id=1, replica_groups=mesh['tm'=2,'space'=16] {'tm','space'}, use_global_device_ids=true, to_apply=%region_1.2 | all-reduce | flops 2 | bytes 16 | tf_op jit(solution)/shard_map/psum | solution.py:76
  167.5 0.9 multiply_subtract_fusion
  (26 shorter events, 0.3 us)
Async XLA Ops:
  9.6 13.0 %copy-start.3 = (s32[2,2048]{1,0:T(2,128)S(1)}, s32[2,2048]{1,0:T(2,128)}, u32[]{:S(2)}) copy-start(s32[2,2048]{1,0:T(2,128)} %param.10) | copy-start | bytes 49156
  9.6 13.1 %copy-start.7 = (s32[2]{0:T(128)S(1)}, s32[2]{0:T(128)}, u32[]{:S(2)}) copy-start(s32[2]{0:T(128)} %constant.15) | copy-start | bytes 28
  9.6 13.2 %copy-start.8 = (s32[2]{0:T(128)S(1)}, s32[2]{0:T(128)}, u32[]{:S(2)}) copy-start(s32[2]{0:T(128)} %constant.61) | copy-start | bytes 28
  13.4 20.5 %copy-start = (bf16[2,32,4,3200]{3,2,1,0:T(4,128)(2,1)S(1)}, bf16[2,32,4,3200]{3,2,1,0:T(4,128)(2,1)}, u32[]{:S(2)}) copy-start(bf16[2,32,4,3200]{3,2,1,0:T(4,128)(2,1)} %param.9) | copy-start | bytes 4915204
  16.3 11.6 %all-to-all-start = ((bf16[16,2,1600]{2,1,0:T(2,128)(2,1)}), bf16[16,2,1600]{2,1,0:T(2,128)(2,1)S(1)}, u32[]{:S(2)}, u32[]{:S(2)}) async-start(bf16[16,2,1600]{2,1,0:T(2,128)(2,1)} %reshape.139), calls=%async_computation | async-start | bytes 212992 | tf_op jit(solution)/shard_map/all_to_all | solution.py:45
  22.6 81.7 %reduce-scatter.2.cloned.1.call-start = ((), (), s32[]{:S(2)}) async-start(), calls=%async_computation.3 | async-start | bytes 307200 | tf_op jit(solution)/shard_map/reduce_scatter | solution.py:63
  34.9 35.0 %copy-start.4 = (f32[2,2048]{1,0:T(2,128)S(1)}, f32[2,2048]{1,0:T(2,128)}, u32[]{:S(2)}) copy-start(f32[2,2048]{1,0:T(2,128)} %param.12) | copy-start | bytes 49156
  34.9 35.0 %copy-start.5 = (f32[2,2048]{1,0:T(2,128)S(1)}, f32[2,2048]{1,0:T(2,128)}, u32[]{:S(2)}) copy-start(f32[2,2048]{1,0:T(2,128)} %param.11) | copy-start | bytes 49156
  34.9 35.0 %copy-start.6 = (s32[2,2048]{1,0:T(2,128)S(1)}, s32[2,2048]{1,0:T(2,128)}, u32[]{:S(2)}) copy-start(s32[2,2048]{1,0:T(2,128)} %param.13) | copy-start | bytes 49156
  106.6 16.4 %copy-start.2 = (f32[51200]{0:T(1024)S(1)}, f32[51200]{0:T(1024)}, u32[]{:S(2)}) copy-start(f32[51200]{0:T(1024)} %param.8) | copy-start | bytes 614404
  106.6 11.5 %all-to-all-start.1 = ((bf16[16,2,1600]{2,1,0:T(2,128)(2,1)}), bf16[16,2,1600]{2,1,0:T(2,128)(2,1)S(1)}, u32[]{:S(2)}, u32[]{:S(2)}) async-start(bf16[16,2,1600]{2,1,0:T(2,128)(2,1)} %reshape.141), calls=%async_computation.2 | async-start | bytes 212992 | tf_op jit(solution)/shard_map/all_to_all | solution.py:71
  118.3 4.8 %copy-start.1 = (f32[1,51200]{1,0:T(1,128)S(1)}, f32[1,51200]{1,0:T(1,128)}, u32[]{:S(2)}) copy-start(f32[1,51200]{1,0:T(1,128)} %param.7) | copy-start | bytes 614404
Sparse Core Ops, SparseCore 0:
  95.0 9.2 reduce-scatter.1
where the time goes:
time: 176 us; the launch traced here: 175 us
  blocking collectives  47.9 us (27%)
  local copies, waits for them, and re-layouts  38.5 us (22%)
  other arithmetic  33.7 us (19%)
  waiting for transfers between devices  18.3 us (10%)
  between operations  17 us (10%)
  starting transfers between devices  12.5 us (7%)
  matrix products  7.25 us (4%)
    psum x1, blocking collectives, per_device(): obs_cost, back_cost = lax.psum((obs_part, back_part), ('tm', 'space'))  42.1 us
    gather x3, local copies, waits for them, and re-layouts, per_device(): modelled = jnp.take_along_axis(cells_flat, obs_index, axis=1)  34.9 us
    unnamed x9, other arithmetic  23.4 us
    reduce_scatter x1, waiting for transfers between devices, per_device(): lax.psum_scatter(jnp.einsum('qiyr,qyr->ir', selected_entries, control_upd...  9.45 us
    all_to_all x1, starting transfers between devices, per_device(): lax.all_to_all(member_field, 'space', split_axis=1, concat_axis=0, tiled=...  6.27 us
    all_to_all x1, starting transfers between devices, per_device(): lax.all_to_all(summed_rows.astype(jnp.bfloat16), 'space', split_axis=0, c...  6.2 us
    all_gather x1, blocking collectives, per_device(): lax.all_gather(pieces, 'tm', axis=0, tiled=True)  5.84 us
    all_to_all x1, waiting for transfers between devices, per_device(): lax.all_to_all(member_field, 'space', split_axis=1, concat_axis=0, tiled=...  4.91 us
  transfers between devices with their start and end apart: 3, of which 3 were waited for; matrix products, arithmetic and copies ran while one was open for 0% of the time, Pallas kernels for 0%

commit v1 on v0

--- a/solution.py
+++ b/solution.py
@@ -1,3 +1,4 @@
+import functools
 import jax
 import jax.numpy as jnp
 from jax import lax
@@ -5,6 +6,15 @@
 
 GX = 320
 GY = 160
+
+
+def group_view(incoming_x, axis_id, chip_axis):
+    for dev_j in (axis_id, chip_axis):
+        incoming_x = lax.psum(incoming_x, dev_j)
+    return incoming_x
+
+
+_post_inputs = functools.partial(group_view, axis_id="space", chip_axis="tm")
 
 
 def lookup_tables(segment_length):
@@ -73,7 +83,7 @@
     ).astype(summed_rows.dtype)
     gradient = control + analyze(adjoint, spectrum, basis_x, basis_y)
     grad_part = jnp.sum(gradient * gradient)
-    obs_cost, back_cost = lax.psum((obs_part, back_part), ("tm", "space"))
+    obs_cost, back_cost = _post_inputs((obs_part, back_part))
     grad_sq = lax.psum(grad_part, ("tm", "space"))
     total_cost = back_cost + obs_cost
     step_size = 0.5 * total_cost / (grad_sq + 1e-06)

time: 176 us -> 210 us (1.19)
  blocking collectives: 47.9 us -> 85.7 us
  waiting for transfers between devices: 18.3 us -> 14.4 us
    psum x1 -> x3, blocking collectives: 42.1 us -> 79.9 us  [the longest x1 48.2 us: per_device(): grad_sq = lax.psum(grad_part, ('tm', 'space'))]
    all_to_all x1, waiting for transfers between devices: 3.95 us -> 0.01 us  [per_device(): lax.all_to_all(summed_rows.astype(jnp.bfloat16), 'space', split_axis=0, c...]
  transfers between devices with their start and end apart: 3 -> 3, of which waited for: 3 -> 2; matrix products, arithmetic and copies ran while one was open for 0% -> 0% of each run, Pallas kernels for 0% -> 0%
where the time goes in v1:
time: 210 us; the launch traced here: 209 us
  blocking collectives  85.7 us (41%)
  local copies, waits for them, and re-layouts  38.5 us (18%)
  other arithmetic  33.7 us (16%)
  between operations  17 us (8%)
  waiting for transfers between devices  14.4 us (7%)
  starting transfers between devices  12.5 us (6%)
  matrix products  7.25 us (3%)
    psum x1, blocking collectives, per_device(): grad_sq = lax.psum(grad_part, ('tm', 'space'))  48.2 us
    gather x3, local copies, waits for them, and re-layouts, per_device(): modelled = jnp.take_along_axis(cells_flat, obs_index, axis=1)  34.9 us
    psum x2, blocking collectives, group_view(): incoming_x = lax.psum(incoming_x, dev_j)  31.7 us
    unnamed x9, other arithmetic  23.4 us
    reduce_scatter x1, waiting for transfers between devices, per_device(): lax.psum_scatter(jnp.einsum('qiyr,qyr->ir', selected_entries, control_upd...  9.45 us
    all_to_all x1, starting transfers between devices, per_device(): lax.all_to_all(member_field, 'space', split_axis=1, concat_axis=0, tiled=...  6.27 us
    all_to_all x1, starting transfers between devices, per_device(): lax.all_to_all(summed_rows.astype(jnp.bfloat16), 'space', split_axis=0, c...  6.2 us
    all_gather x1, blocking collectives, per_device(): lax.all_gather(pieces, 'tm', axis=0, tiled=True)  5.84 us
  transfers between devices with their start and end apart: 3, of which 2 were waited for; matrix products, arithmetic and copies ran while one was open for 0% of the time, Pallas kernels for 0%

profile of v1, /device:TPU:12, one launch (start us, length us, event | category | flops | bytes accessed | tf_op | source)
XLA Modules:
  0.0 209.1 jit_solution(17337884691341287149)
XLA Ops:
  7.2 2.4 %multiply_reduce_fusion.4 = (f32[]{:T(128)}, f32[51200]{0:T(1024)S(1)}) fusion(f32[1,51200]{1,0:T(1,128)} %param.7, f32[1,51200]{1,0:T(1,128)} %bitcast.56), kind=kLoop, calls=%fused_computation.23 | loop fusion | flops 153599 | bytes 614404 | tf_op jit(solution)/shard_map/reduce_sum | solution.py:68
  9.6 0.1 reshape.98
  9.8 2.6 %convolution_bitcast_fusion.1 = f32[320,160]{0,1:T(8,128)S(1)} fusion(f32[320,160]{1,0:T(8,128)S(1)} %reshape.98, f32[320]{0:T(512)S(1)} %add_multiply_fusion, pred[320]{0:T(512)(128)(4,1)S(1)} %iota_compare_fusion), kind=kOutput, calls=%fused_computation.5 | convolution fusion | flops 197120000 | bytes 411200 | tf_op jit(solution)/shard_map/kn,mkl->mnl/dot_general | solution.py:31
  12.4 1.1 convolution_convert_fusion
  13.4 0.0 copy-start
  13.5 0.1 copy.14
  13.6 0.3 convert_element_type.33
  13.9 0.5 broadcast.94
  14.4 1.2 reduce.13
  15.5 0.8 reshape.139
  16.3 6.3 %all-to-all-start = ((bf16[16,2,1600]{2,1,0:T(2,128)(2,1)}), bf16[16,2,1600]{2,1,0:T(2,128)(2,1)S(1)}, u32[]{:S(2)}, u32[]{:S(2)}) async-start(bf16[16,2,1600]{2,1,0:T(2,128)(2,1)} %reshape.139), calls=%async_computation | async-start | bytes 212992 | tf_op jit(solution)/shard_map/all_to_all | solution.py:55
  22.6 0.0 reduce-scatter.2.cloned.1.call-start
  22.7 0.0 copy-done.3
  22.7 0.0 copy-done.7
  22.7 0.1 multiply_reduce_fusion.5
  22.8 0.0 copy-done.8
  22.8 0.1 and_reduce_fusion
  23.0 4.9 %all-to-all-done = bf16[16,2,1600]{2,1,0:T(2,128)(2,1)S(1)} async-done(((bf16[16,2,1600]{2,1,0:T(2,128)(2,1)}), bf16[16,2,1600]{2,1,0:T(2,128)(2,1)S(1)}, u32[]{:S(2)}, u32[]{:S(2)}) %all-to-all-start) | async-done | bytes 102432 | tf_op jit(solution)/shard_map/all_to_all | solution.py:55
  27.9 0.2 reshape.140
  28.1 5.8 %all-gather = bf16[1,32,3200]{2,1,0:T(8,128)(2,1)S(1)} all-gather(bf16[1,16,3200]{2,1,0:T(8,128)(2,1)S(1)} %copy.16), channel_id=2, replica_groups=mesh['tm'=2,'space'=16] {'tm'}, dimensions={1}, use_global_device_ids=true | all-gather | bytes 307200 | tf_op jit(solution)/shard_map/all_gather | solution.py:60
  34.0 0.0 copy-done
  34.0 0.9 multiply_reduce_fusion.1
  34.8 0.1 copy.36
  34.9 0.0 copy-start.4
  34.9 0.0 copy-start.5
  34.9 0.0 copy-start.6
  34.9 34.9 %gather_fusion = f32[4096]{0:T(1024)S(1)} fusion(f32[2,12800]{1,0:T(2,128)S(1)} %bitcast.52, s32[4096]{0:T(1024)S(1)} %bitcast.53), kind=kCustom, calls=%fused_computation | custom fusion | bytes 65536 | tf_op jit(solution)/shard_map/jit(take_along_axis)/gather | solution.py:64
  69.9 0.8 fusion.26
  70.7 21.9 %scatter_custom_fusion = f32[25600]{0:T(1024)S(1)} fusion(s32[4096]{0:T(1024)S(1)} %bitcast.61, f32[4096]{0:T(1024)S(1)} %bitcast.62, f32[]{:T(128)} %constant.17.clone.1), kind=kCustom, calls=%fused_computation.39 | custom fusion | flops 4096 | bytes 102404
  92.7 2.2 %multiply_reduce_fusion = bf16[3200,32]{0,1:T(8,128)(2,1)} fusion(f32[3200,2,4]{0,2,1:T(4,128)S(1)} %bitcast_convert_fusion.1, bf16[2,32,4,3200]{3,2,1,0:T(4,128)(2,1)S(1)} %copy-done), kind=kLoop, calls=%fused_computation.2 | loop fusion | flops 2355200 | bytes 1945600 | tf_op jit(solution)/shard_map/qiyr,qyr->ir/dot_general | solution.py:74
  94.9 0.0 reduce-scatter.2.cloned.1.call-update
  94.9 9.4 %reduce-scatter.2.cloned.1.call-done = bf16[16,3200]{1,0:T(8,128)(2,1)} async-done(((bf16[32,3200]{1,0:T(8,128)(2,1)}), bf16[16,3200]{1,0:T(8,128)(2,1)}) %reduce-scatter.2.cloned.1.call-update) | async-done | bytes 102416 | tf_op jit(solution)/shard_map/reduce_scatter | solution.py:73
  104.3 1.5 reduce.14
  105.8 0.8 reshape.141
  106.6 6.2 %all-to-all-start.1 = ((bf16[16,2,1600]{2,1,0:T(2,128)(2,1)}), bf16[16,2,1600]{2,1,0:T(2,128)(2,1)S(1)}, u32[]{:S(2)}, u32[]{:S(2)}) async-start(bf16[16,2,1600]{2,1,0:T(2,128)(2,1)} %reshape.141), calls=%async_computation.2 | async-start | bytes 212992 | tf_op jit(solution)/shard_map/all_to_all | solution.py:81
  114.2 26.0 %psum.41 = f32[]{:T(128)} all-reduce(f32[]{:T(128)S(6)} %add.69), channel_id=1, replica_groups=mesh['tm'=2,'space'=16] {'space'}, use_global_device_ids=true, to_apply=%region_1.2 | all-reduce | flops 1 | bytes 8 | tf_op jit(solution)/shard_map/psum | solution.py:13
  140.1 5.7 %psum.40 = f32[]{:T(128)} all-reduce(f32[]{:T(128)} %psum.41), channel_id=1, replica_groups=mesh['tm'=2,'space'=16] {'tm'}, use_global_device_ids=true, to_apply=%region_2.3 | all-reduce | flops 1 | bytes 8 | tf_op jit(solution)/shard_map/psum | solution.py:13
  146.5 0.0 all-to-all-done.1
  146.5 0.2 reshape.142
  146.7 0.0 copy-start.1
  146.7 0.6 reduce.5
  147.3 0.2 reshape.103
  147.5 2.3 %convolution_bitcast_fusion = f32[320,160]{0,1:T(8,128)S(1)} fusion(bf16[320,160]{1,0:T(8,128)(2,1)S(1)} %reshape.103, f32[320]{0:T(512)S(1)} %add_multiply_fusion, pred[320]{0:T(512)(128)(4,1)S(1)} %iota_compare_fusion), kind=kOutput, calls=%fused_computation.4 | convolution fusion | flops 197120000 | bytes 308800 | tf_op jit(solution)/shard_map/kn,mnp->mkp/dot_general | solution.py:38
  149.8 1.3 fusion.10
  151.1 0.3 reshape.105
  151.5 1.0 multiply_reduce_fusion.2
  152.5 48.2 %psum.39 = f32[]{:T(128)} all-reduce(f32[]{:T(128)} %get-tuple-element.4), channel_id=1, replica_groups=mesh['tm'=2,'space'=16] {'tm','space'}, use_global_device_ids=true, to_apply=%region_9.10 | all-reduce | flops 1 | bytes 8 | tf_op jit(solution)/shard_map/psum | solution.py:87
  201.4 0.9 multiply_subtract_fusion
  (28 shorter events, 0.3 us)
Async XLA Ops:
  9.6 13.0 %copy-start.3 = (s32[2,2048]{1,0:T(2,128)S(1)}, s32[2,2048]{1,0:T(2,128)}, u32[]{:S(2)}) copy-start(s32[2,2048]{1,0:T(2,128)} %param.10) | copy-start | bytes 49156
  9.6 13.1 %copy-start.7 = (s32[2]{0:T(128)S(1)}, s32[2]{0:T(128)}, u32[]{:S(2)}) copy-start(s32[2]{0:T(128)} %constant.15) | copy-start | bytes 28
  9.6 13.2 %copy-start.8 = (s32[2]{0:T(128)S(1)}, s32[2]{0:T(128)}, u32[]{:S(2)}) copy-start(s32[2]{0:T(128)} %constant.61) | copy-start | bytes 28
  13.4 20.5 %copy-start = (bf16[2,32,4,3200]{3,2,1,0:T(4,128)(2,1)S(1)}, bf16[2,32,4,3200]{3,2,1,0:T(4,128)(2,1)}, u32[]{:S(2)}) copy-start(bf16[2,32,4,3200]{3,2,1,0:T(4,128)(2,1)} %param.9) | copy-start | bytes 4915204
  16.3 11.6 %all-to-all-start = ((bf16[16,2,1600]{2,1,0:T(2,128)(2,1)}), bf16[16,2,1600]{2,1,0:T(2,128)(2,1)S(1)}, u32[]{:S(2)}, u32[]{:S(2)}) async-start(bf16[16,2,1600]{2,1,0:T(2,128)(2,1)} %reshape.139), calls=%async_computation | async-start | bytes 212992 | tf_op jit(solution)/shard_map/all_to_all | solution.py:55
  22.6 81.7 %reduce-scatter.2.cloned.1.call-start = ((), (), s32[]{:S(2)}) async-start(), calls=%async_computation.3 | async-start | bytes 307200 | tf_op jit(solution)/shard_map/reduce_scatter | solution.py:73
  34.9 35.0 %copy-start.4 = (f32[2,2048]{1,0:T(2,128)S(1)}, f32[2,2048]{1,0:T(2,128)}, u32[]{:S(2)}) copy-start(f32[2,2048]{1,0:T(2,128)} %param.12) | copy-start | bytes 49156
  34.9 35.0 %copy-start.5 = (f32[2,2048]{1,0:T(2,128)S(1)}, f32[2,2048]{1,0:T(2,128)}, u32[]{:S(2)}) copy-start(f32[2,2048]{1,0:T(2,128)} %param.11) | copy-start | bytes 49156
  34.9 35.0 %copy-start.6 = (s32[2,2048]{1,0:T(2,128)S(1)}, s32[2,2048]{1,0:T(2,128)}, u32[]{:S(2)}) copy-start(s32[2,2048]{1,0:T(2,128)} %param.13) | copy-start | bytes 49156
  106.6 44.8 %copy-start.2 = (f32[51200]{0:T(1024)S(1)}, f32[51200]{0:T(1024)}, u32[]{:S(2)}) copy-start(f32[51200]{0:T(1024)} %param.8) | copy-start | bytes 614404
  106.6 39.9 %all-to-all-start.1 = ((bf16[16,2,1600]{2,1,0:T(2,128)(2,1)}), bf16[16,2,1600]{2,1,0:T(2,128)(2,1)S(1)}, u32[]{:S(2)}, u32[]{:S(2)}) async-start(bf16[16,2,1600]{2,1,0:T(2,128)(2,1)} %reshape.141), calls=%async_computation.2 | async-start | bytes 212992 | tf_op jit(solution)/shard_map/all_to_all | solution.py:81
  146.7 4.7 %copy-start.1 = (f32[1,51200]{1,0:T(1,128)S(1)}, f32[1,51200]{1,0:T(1,128)}, u32[]{:S(2)}) copy-start(f32[1,51200]{1,0:T(1,128)} %param.7) | copy-start | bytes 614404
Sparse Core Ops, SparseCore 0:
  95.0 9.2 reduce-scatter.1
